TPU v7x, 256 devices: a whole 4x4x8 slice. The times are simulated.
256 devices in a mesh: section: 64 (over z, x, core), atlas: 4 (over y).
Axes of the slice: x: 4, y: 4, z: 8, core: 2. Of those that a mesh axis runs over, the one named last changes fastest.
Arguments:
- counts: bfloat16 [131072, 5120], P(('section', 'atlas')), may hold values from -24 to 24
- gene_scale: float32 [5120], replicated, may hold values from 0.3 to 3
- cell_scale: float32 [131072], P(('section', 'atlas')), may hold values from 1 to 48
- gene_basis: bfloat16 [5120, 256], replicated, may hold values from -0.078125 to 0.078125
Outputs:
- cell_basis: bfloat16 [131072, 256], P(('section', 'atlas'))
- gene_side: float32 [5120, 256], P(('section', 'atlas'))
All inputs are finite; a program needn't handle non-finite values.
Results may differ from a plain program's by a relative error of at most 0.0051.
Values sent between devices are 32-bit elements; how exact they have to be, the bound alone decides.
A program may use at most 64 MiB of HBM per device.

v0:
```python
import jax
import jax.numpy as jnp
from jax import lax
from jax.sharding import PartitionSpec as P


def local(counts, gene_scale, cell_scale, gene_basis):
    highest = lax.Precision.HIGHEST
    device_count = lax.axis_size("section") * lax.axis_size("atlas")
    cells_all = counts.shape[0] * device_count
    gene_count = counts.shape[1]
    scaled = (gene_basis.astype(jnp.float32) * gene_scale[:, None]).astype(jnp.bfloat16)
    sketch = jnp.dot(counts, scaled, preferred_element_type=jnp.float32) * cell_scale[:, None]
    weighted = (sketch * cell_scale[:, None]).astype(jnp.bfloat16)
    gene_sums = lax.psum_scatter(
        lax.dot_general(
            counts, weighted, (((0,), (0,)), ((), ())), preferred_element_type=jnp.float32
        ),
        ("section", "atlas"),
        scatter_dimension=0,
        tiled=True,
    )
    gram_local = (
        jnp.dot(sketch.T, sketch, precision=highest, preferred_element_type=jnp.float32) / cells_all
    )
    gram_total = lax.psum(gram_local, ("section", "atlas"))
    lower_factor = jnp.linalg.cholesky(gram_total)
    identity_matrix = jnp.eye(sketch.shape[1], dtype=jnp.float32)
    inverse = jax.scipy.linalg.solve_triangular(lower_factor, identity_matrix, lower=True)
    orthonormal = jnp.dot(sketch, inverse.T, precision=highest, preferred_element_type=jnp.float32)
    cell_basis = orthonormal.astype(jnp.bfloat16)
    rows_mine = gene_count // device_count
    position = lax.axis_index("section") * lax.axis_size("atlas") + lax.axis_index("atlas")
    own_scale = lax.dynamic_slice_in_dim(gene_scale, position * rows_mine, rows_mine)
    rotated = jnp.dot(gene_sums, inverse.T, precision=highest, preferred_element_type=jnp.float32)
    gene_side = rotated * (own_scale / cells_all)[:, None]
    return (cell_basis, gene_side)


def solution(mesh):
    return jax.shard_map(
        local,
        mesh=mesh,
        in_specs=(P(("section", "atlas"), None), P(), P(("section", "atlas")), P()),
        out_specs=(P(("section", "atlas"), None), P(("section", "atlas"), None)),
        check_vma=False,
    )
```

profile of v0, /device:TPU:1, one launch (start us, length us, event | category | flops | bytes accessed | tf_op | source)
XLA Modules:
  0.0 367.4 jit_solution(12759801630752260313)
XLA Ops:
  7.2 0.0 copy-start.1
  7.2 0.0 all-reduce.5.cloned.1.call-start
  7.2 0.0 copy-start
  7.2 5.8 %fusion.2 = f32[256,512]{1,0:T(8,128)S(1)} fusion(bf16[512,5120]{1,0:T(8,128)(2,1)} %param.4, bf16[5120,256]{1,0:T(8,128)(2,1)} %param.7, f32[5120]{0:T(1024)} %param.5, f32[512]{0:T(512)} %param.6), kind=kOutput, calls=%fused_computation.6 | convolution fusion | flops 1346240512 | bytes 8411136 | tf_op jit(solution)/shard_map/dot_general | solution.py:13
  13.0 0.0 copy-done.1
  13.0 0.0 copy-done
  13.0 3.9 %convolution_bitcast_fusion = f32[5120,256]{0,1:T(8,128)} fusion(bf16[512,5120]{1,0:T(8,128)(2,1)S(1)} %copy-done, f32[256,512]{1,0:T(8,128)S(1)} %fusion.2, f32[512]{0:T(512)S(1)} %copy-done.1), kind=kOutput, calls=%fused_computation.2 | convolution fusion | flops 1342439424 | bytes 11012096 | tf_op jit(solution)/shard_map/dot_general | solution.py:16
  16.9 1.3 convolution_multiply_fusion
  18.3 0.0 all-reduce.5.cloned.1.call-update
  18.3 0.8 dynamic-slice_multiply_fusion
  19.1 275.1 %all-reduce.5.cloned.1.call-done = (f32[256,256]{0,1:T(8,128)}, f32[5120,256]{0,1:T(8,128)}) async-done(((f32[256,256]{0,1:T(8,128)}, f32[5120,256]{0,1:T(8,128)}), (f32[256,256]{0,1:T(8,128)}, f32[5120,256]{0,1:T(8,128)})) %all-reduce.5.cloned.1.call-update) | async-done | bytes 5505040 | tf_op jit(solution)/shard_map/psum | solution.py:26
  294.2 1.1 copy.9
  295.3 1.0 fusion.3
  296.3 11.7 %cholesky.50 = f32[128,128]{1,0:T(8,128)S(1)} custom-call(f32[128,128]{1,0:T(8,128)S(1)} %cholesky.118), custom_call_target="Cholesky" | custom-call | tf_op jit(solution)/shard_map/jit(cholesky)/cholesky | solution.py:27
  308.0 9.8 %custom-call.15 = f32[1,128,128]{1,2,0:T(8,128)S(1)} custom-call(f32[1,128,128]{2,1,0:T(8,128)S(1)} %get-tuple-element.25), custom_call_target="InvertDiagBlocksLowerTriangular" | custom-call | tf_op jit(solution)/shard_map/jit(cholesky)/cholesky | solution.py:27
  317.9 0.2 constant_dynamic-update-slice_fusion.1
  318.1 0.3 convolution_subtract_fusion.1
  318.3 11.9 %cholesky.105 = f32[128,128]{1,0:T(8,128)S(1)} custom-call(f32[128,128]{1,0:T(8,128)S(1)} %convolution_subtract_fusion.1), custom_call_target="Cholesky" | custom-call | tf_op jit(solution)/shard_map/jit(cholesky)/cholesky | solution.py:27
  330.3 0.7 compare_reduce_fusion
  332.2 0.1 triangular_solve.63
  332.3 4.0 %while.1 = (s32[]{:T(128)}, f32[256,256]{1,0:T(8,128)S(1)}, s32[2,2]{1,0:T(2,128)S(1)}, f32[2,128,128]{2,1,0:T(8,128)S(1)}, s32[]{:T(128)}) while((s32[]{:T(128)}, f32[256,256]{1,0:T(8,128)S(1)}, s32[2,2]{1,0:T(2,128)S(1)}, f32[2,128,128]{2,1,0:T(8,128)S(1)}, s32[]{:T(128)}) %tuple.27), condition=%wide.while_cond, body=%wide.while_body.sunk | while | flops 2 | bytes 131181 | solution.py:29
  332.3 0.6 fusion.27
  332.9 1.4 bitcast_dynamic-update-slice_fusion.2
  334.3 0.6 fusion.27
  334.9 1.4 bitcast_dynamic-update-slice_fusion.2
  336.3 19.7 %custom-call.16 = f32[2,128,128]{1,2,0:T(8,128)S(1)} custom-call(f32[2,128,128]{2,1,0:T(8,128)S(1)} %get-tuple-element.9), custom_call_target="InvertDiagBlocksLowerTriangular" | custom-call | tf_op jit(solution)/shard_map/jit(_solve_triangular)/triangular_solve | solution.py:29
  356.0 0.3 fusion.6
  356.2 0.3 convolution_subtract_fusion
  356.5 0.3 fusion.9
  356.8 1.7 convolution_convert_fusion
  358.5 2.0 convolution_multiply_fusion.1
  (10 shorter events, 0.2 us)
Async XLA Ops:
  7.2 5.8 %copy-start.1 = (f32[512]{0:T(512)S(1)}, f32[512]{0:T(512)}, u32[]{:S(2)}) copy-start(f32[512]{0:T(512)} %param.6) | copy-start | bytes 6148
  7.2 287.0 %all-reduce.5.cloned.1.call-start = ((), (), s32[]{:S(2)}) async-start(), calls=%async_computation | async-start | bytes 11010048 | tf_op jit(solution)/shard_map/psum | solution.py:26
  7.2 5.8 %copy-start = (bf16[512,5120]{1,0:T(8,128)(2,1)S(1)}, bf16[512,5120]{1,0:T(8,128)(2,1)}, u32[]{:S(2)}) copy-start(bf16[512,5120]{1,0:T(8,128)(2,1)} %param.4) | copy-start | bytes 15728644
Sparse Core Ops, SparseCore 0:
  18.4 275.7 all-reduce.4
where the time goes:
time: 369 us; the launch traced here: 367 us
  waiting for transfers between devices  275 us (75%)
  other arithmetic  55.7 us (15%)
  matrix products  16 us (4%)
  between operations  15.5 us (4%)
  local copies, waits for them, and re-layouts  5.11 us (1%)
    psum x1, waiting for transfers between devices, local(): gram_total = lax.psum(gram_local, ('section', 'atlas'))  275 us
    another operation x6, other arithmetic, local(): lower_factor = jnp.linalg.cholesky(gram_total)  34.1 us
    another operation x3, other arithmetic, local(): jax.scipy.linalg.solve_triangular(lower_factor, identity_matrix, lower=True)  19.7 us
  transfers between devices with their start and end apart: 1, of which 1 were waited for; matrix products, arithmetic and copies ran while one was open for 0% of the time, Pallas kernels for 0%

commit v1 on v0

v1 whole, which is shorter than its diff:
```python
import functools

import jax
import jax.numpy as jnp
from jax import lax
from jax.experimental import pallas as pl
from jax.experimental.pallas import tpu as pltpu
from jax.sharding import PartitionSpec as P

HI = lax.Precision.HIGHEST
F32 = jnp.float32

def _sub(x, j):
    return jnp.broadcast_to(x[j:j + 1, :], x.shape)

def sweep(C, sub):
    C = list(C)
    Wt = [jnp.zeros((8, 128), F32) for _ in range(8)]
    piv = jnp.ones((8, 128), F32)
    for j in range(0, 8, 2):
        a, b, c = _sub(C[j], j), _sub(C[j], j + 1), _sub(C[j + 1], j + 1)
        r = 1.0 / (a * c - b * b)
        i11, i12, i22 = c * r, -b * r, a * r
        ra = 1.0 / a
        e = b * ra
        piv = jnp.where(sub == j, a, jnp.where(sub == j + 1, c - b * e, piv))
        for k in range(j):
            low = C[k] - e * _sub(C[k], j)
            Wt[k] = jnp.where(sub == j, C[k], jnp.where(sub == j + 1, low, Wt[k]))
        Wt[j] = jnp.where(sub == j, 1.0, jnp.where(sub == j + 1, -e, Wt[j]))
        Wt[j + 1] = jnp.where(sub == j + 1, 1.0, Wt[j + 1])
        for k in range(8):
            if k not in (j, j + 1):
                q0, q1 = _sub(C[k], j), _sub(C[k], j + 1)
                s0 = i11 * q0 + i12 * q1
                s1 = i12 * q0 + i22 * q1
                new = C[k] - (C[j] * s0 + C[j + 1] * s1)
                C[k] = jnp.where(sub == j, s0, jnp.where(sub == j + 1, s1, new))
        x, y = C[j], C[j + 1]
        C[j] = jnp.where(sub == j, i11, jnp.where(sub == j + 1, i12, -(x * i11 + y * i12)))
        C[j + 1] = jnp.where(sub == j, i12, jnp.where(sub == j + 1, i22, -(x * i12 + y * i22)))
    rs = lax.rsqrt(piv)
    return C, [w * rs for w in Wt]

def tree(xs):
    xs = list(xs)
    while len(xs) > 1:
        xs = [xs[i] + xs[i + 1] if i + 1 < len(xs) else xs[i] for i in range(0, len(xs), 2)]
    return xs[0]

def invchol128(M):
    n = len(M)
    M = list(M)
    sub = lax.broadcasted_iota(jnp.int32, (8, 128), 0)
    lane = lax.broadcasted_iota(jnp.int32, (8, 128), 1)
    out = []
    for k in range(n):
        blk = (lane >= 8 * k) & (lane < 8 * k + 8)
        Cb = [[jnp.broadcast_to(M[i][:, 8 * k + u:8 * k + u + 1], (8, 128)) for u in range(8)] for i in range(k, n)]
        m = jnp.where(blk, jnp.where(lane == 8 * k + sub, 1.0, 0.0), M[k])
        mb = [_sub(m, u) for u in range(8)]
        P, W8 = sweep(Cb[0], sub)
        T = tree([P[u] * mb[u] for u in range(8)])
        Tb = [_sub(T, u) for u in range(8)]
        for i in range(k + 1, n):
            M[i] = jnp.where(blk, 0.0, M[i]) - tree([Cb[i - k][u] * Tb[u] for u in range(8)])
        row = tree([W8[u] * mb[u] for u in range(8)])
        out.append(jnp.where(lane < 8 * k + 8, row, 0.0))
    return out

def dot(a, b, dims=((1,), (0,))):
    return lax.dot_general(a, b, (dims, ((), ())), precision=HI, preferred_element_type=F32)

def invchol256(g, w, between):
    o = invchol128([g[8 * i:8 * i + 8, 0:128] for i in range(16)])
    for i in range(16):
        w[8 * i:8 * i + 8, 0:128] = o[i]
        w[8 * i:8 * i + 8, 128:256] = jnp.zeros((8, 128), F32)
    w11 = w[0:128, 0:128]
    l21 = dot(g[128:256, 0:128], w11, ((1,), (1,)))
    g[128:256, 128:256] = g[128:256, 128:256] - dot(l21, l21, ((1,), (1,)))
    g[128:256, 0:128] = dot(l21, w11)
    between()
    o = invchol128([g[128 + 8 * i:136 + 8 * i, 128:256] for i in range(16)])
    for i in range(16):
        w[128 + 8 * i:136 + 8 * i, 128:256] = o[i]
    w[128:256, 0:128] = -dot(w[128:256, 128:256], g[128:256, 0:128])


MESH = pl.DeviceIdType.MESH
NZ, NX, NY = 8, 4, 4
PLANE = NX * NY * 2
CHUNKS = 10


def _wait(view, sem):
    pltpu.make_async_copy(view, view, sem).wait()


def _column(rows):
    r = rows.shape[0]
    return jnp.concatenate([rows, jnp.zeros((128 - r, 128), F32)], axis=0).T


class Ring4:
    def __init__(self, block, i, ids, plus, minus, sems, out):
        self.block, self.plus, self.minus, self.sems, self.out = block, plus, minus, sems, out
        self.i, self.ids = i, ids
        self.up, self.down, self.far = lax.rem(i + 1, 4), lax.rem(i + 3, 4), lax.rem(i + 2, 4)

    def send(self, q, owner, forward, slot):
        buf = self.plus if forward else self.minus
        pltpu.make_async_remote_copy(
            src_ref=self.block(q, owner),
            dst_ref=buf.at[slot],
            send_sem=self.sems.at[6 if forward else 7],
            recv_sem=self.sems.at[slot if forward else 3 + slot],
            device_id=self.ids(self.up if forward else self.down),
            device_id_type=MESH,
        ).start()

    def start(self):
        self.send(0, self.far, True, 0)
        self.send(1, self.far, False, 0)
        self.send(1, self.up, True, 1)
        self.send(0, self.down, False, 1)

    def middle(self):
        _wait(self.plus.at[0], self.sems.at[0])
        ref = self.block(0, self.up)
        ref[...] = ref[...] + self.plus[0]
        self.send(0, self.up, True, 2)
        _wait(self.minus.at[0], self.sems.at[3])
        ref = self.block(1, self.down)
        ref[...] = ref[...] + self.minus[0]
        self.send(1, self.down, False, 2)

    def finish(self):
        for s in (1, 2):
            _wait(self.plus.at[s], self.sems.at[s])
            _wait(self.minus.at[s], self.sems.at[3 + s])
        self.out[0] = self.block(0, self.i)[...] + (self.plus[2] + self.minus[1])
        self.out[1] = self.block(1, self.i)[...] + (self.plus[1] + self.minus[2])

    def drain(self):
        _wait(self.plus, self.sems.at[6])
        _wait(self.minus, self.sems.at[7])


def kernel(cells_all, counts, basis, scale, cells, cell_basis, gene_side,
           cbuf, bbuf, sbc, sk, wt, gl, gr, gp, zr, gz, gfull, g2, w, stg, S, R,
           XP, XM, YP, YM, PX, PY, X2P, X2M, Y2P, Y2M, Q, zs, z3,
           load_sem, gsem, csem, rsem, zsem):
    sec = lax.axis_index("section")
    y = lax.axis_index("atlas")
    c = lax.rem(sec, 2)
    x = lax.rem(sec // 2, NX)
    z = sec // (2 * NX)
    p = (x * NY + y) * 2 + c

    def plane_id(q):
        return ((z * NX + q // (2 * NY)) * 2 + lax.rem(q, 2), lax.rem(q // 2, NY))

    def z_id(k):
        return ((k * NX + x) * 2 + c, y)

    def x_id(k):
        return ((z * NX + k) * 2 + c, y)

    def y_id(k):
        return (sec, k)

    partner = (sec + 1 - 2 * c, y)
    step = counts.shape[1] // CHUNKS

    def loads(k):
        cols = pl.ds(pl.multiple_of(k * step, step), step)
        return (pltpu.make_async_copy(counts.at[:, cols], cbuf.at[:, cols], load_sem.at[0, k]),
                pltpu.make_async_copy(basis.at[cols, :], bbuf.at[cols, :], load_sem.at[1, k]))

    for k in range(CHUNKS):
        for copy in loads(k):
            copy.start()

    barrier = pltpu.get_barrier_semaphore()

    @pl.loop(1, PLANE)
    def _(d):
        pl.semaphore_signal(barrier, inc=1, device_id=plane_id(lax.rem(p + d, PLANE)), device_id_type=MESH)

    @pl.loop(1, NZ)
    def _(d):
        pl.semaphore_signal(barrier, inc=1, device_id=z_id(lax.rem(z + d, NZ)), device_id_type=MESH)

    turned = _column(scale[...])
    for g in range(scale.shape[0]):
        sbc[128 * g:128 * g + 128, :] = jnp.broadcast_to(turned[:, g:g + 1], (128, 128))

    sk[...] = jnp.zeros_like(sk)

    @pl.loop(0, CHUNKS)
    def _(k):
        for copy in loads(k):
            copy.wait()
        rows = pl.ds(pl.multiple_of(k * step, step), step)
        factor = sbc[rows, :]
        part = bbuf[rows, :].astype(F32)
        scaled = jnp.concatenate([part[:, :128] * factor, part[:, 128:] * factor], axis=1).astype(jnp.bfloat16)
        sk[...] += jnp.dot(cbuf[:, rows], scaled, preferred_element_type=F32)

    turned = _column(cells[...])
    for r in range(cells.shape[0]):
        rows = slice(128 * r, 128 * r + 128)
        factor = jnp.broadcast_to(turned[:, r:r + 1], (128, 256))
        value = sk[rows, :] * factor
        sk[rows, :] = value
        wt[rows, :] = (value * factor).astype(jnp.bfloat16)

    gram = dot(sk[...], sk[...], ((0,), (0,))) * (1.0 / cells_all)
    gl[...] = gram.reshape(PLANE, 8, 256)

    pl.semaphore_wait(barrier, PLANE - 1 + NZ - 1)

    @pl.loop(1, PLANE)
    def _(d):
        q = lax.rem(p + d, PLANE)
        pltpu.make_async_remote_copy(
            src_ref=gl.at[q], dst_ref=gr.at[d - 1], send_sem=gsem.at[0], recv_sem=gsem.at[1],
            device_id=plane_id(q), device_id_type=MESH).start()

    @pl.loop(0, NZ)
    def _(k):
        cols = pl.ds(pl.multiple_of(k * 640, 640), 640)
        part = lax.dot_general(cbuf[:, cols], wt[...], (((0,), (0,)), ((), ())), preferred_element_type=F32)
        factor = sbc[cols, :] * (1.0 / cells_all)
        stg[:, :128] = part[:, :128] * factor
        stg[:, 128:] = part[:, 128:] * factor
        for a in range(NX):
            for b in range(2):
                for e in range(NY):
                    o = ((a * 2 + b) * NY + e) * 20
                    S[b, 0, k, a, e] = stg[o:o + 8, :128]
                    S[b, 1, k, a, e] = stg[o:o + 8, 128:]
                    S[b, 2, k, a, e] = stg[o + 8:o + 16, :128]
                    S[b, 3, k, a, e] = stg[o + 8:o + 16, 128:]
                    S[b, k // 2, 8 + lax.rem(k, 2), a, e] = jnp.concatenate(
                        [stg[o + 16:o + 20, :128], stg[o + 16:o + 20, 128:]], axis=0)
        pltpu.make_async_remote_copy(
            src_ref=S.at[1 - c, :, k], dst_ref=R.at[:, k], send_sem=csem.at[0], recv_sem=csem.at[1],
            device_id=partner, device_id_type=MESH).start()

    pltpu.make_async_remote_copy(
        src_ref=S.at[1 - c, :, 8:10], dst_ref=R.at[:, 8:10], send_sem=csem.at[0], recv_sem=csem.at[1],
        device_id=partner, device_id_type=MESH).start()

    _wait(gr, gsem.at[1])
    gp[...] = gl[p] + jnp.sum(gr[...], axis=0)

    @pl.loop(1, NZ)
    def _(d):
        pltpu.make_async_remote_copy(
            src_ref=gp, dst_ref=zr.at[d - 1], send_sem=gsem.at[2], recv_sem=gsem.at[3],
            device_id=z_id(lax.rem(z + d, NZ)), device_id_type=MESH).start()

    _wait(R, csem.at[1])

    @pl.loop(0, 10)
    def _(u):
        for q in range(4):
            R[q, u] = R[q, u] + S[c, q, u]

    first = Ring4(lambda q, o: R.at[q, :, o], x, x_id, XP, XM, rsem.at[0], PX)
    second = Ring4(lambda q, o: R.at[2 + q, :, :, o], y, y_id, YP, YM, rsem.at[1], PY)
    first.start()
    second.start()

    _wait(zr, gsem.at[3])
    gz[...] = gp[...] + jnp.sum(zr[...], axis=0)
    gfull[p] = gz[...]

    @pl.loop(1, PLANE)
    def _(d):
        pltpu.make_async_remote_copy(
            src_ref=gz, dst_ref=gfull.at[p], send_sem=gsem.at[4], recv_sem=gsem.at[5],
            device_id=plane_id(lax.rem(p + d, PLANE)), device_id_type=MESH).start()

    first.middle()
    second.middle()

    _wait(gfull.at[0:PLANE - 1], gsem.at[5])
    g2[...] = gfull[...].reshape(256, 256)

    third = Ring4(lambda q, o: PX.at[q, :, o], y, y_id, X2P, X2M, rsem.at[2], Q.at[0:2])
    fourth = Ring4(lambda q, o: PY.at[q, :, o], x, x_id, Y2P, Y2M, rsem.at[3], Q.at[2:4])

    def after_half():
        first.finish()
        second.finish()
        third.start()
        fourth.start()
        third.middle()
        fourth.middle()

    invchol256(g2, w, after_half)

    third.finish()
    fourth.finish()
    for k in range(NZ):
        for t in range(4):
            zs[k, t] = Q[t, k]
        zs[k, 4] = Q[k // 2, 8 + k % 2]

    @pl.loop(1, NZ)
    def _(d):
        k = lax.rem(z + d, NZ)
        pltpu.make_async_remote_copy(
            src_ref=zs.at[k], dst_ref=z3.at[d - 1], send_sem=zsem.at[0], recv_sem=zsem.at[1],
            device_id=z_id(k), device_id_type=MESH).start()

    cell_basis[...] = dot(sk[...], w[...], ((1,), (1,))).astype(jnp.bfloat16)

    _wait(z3, zsem.at[1])
    own = zs[z] + jnp.sum(z3[...], axis=0)
    top = jnp.concatenate([own[0], own[1]], axis=1)
    mid = jnp.concatenate([own[2], own[3]], axis=1)
    low = jnp.concatenate([own[4], pltpu.roll(own[4], 4, 0)], axis=1)
    side = dot(jnp.concatenate([top, mid, low], axis=0), w[...], ((1,), (1,)))
    gene_side[...] = side[:20]

    _wait(gr, gsem.at[0])
    _wait(zr, gsem.at[2])
    _wait(gfull.at[0:PLANE - 1], gsem.at[4])
    _wait(R, csem.at[0])
    for ring in (first, second, third, fourth):
        ring.drain()
    _wait(z3, zsem.at[0])


def local(counts, gene_scale, cell_scale, gene_basis):
    device_count = lax.axis_size("section") * lax.axis_size("atlas")
    rows, genes = counts.shape
    vm = lambda *s: pltpu.VMEM(s, F32)
    dma = pltpu.SemaphoreType.DMA
    return pl.pallas_call(
        functools.partial(kernel, rows * device_count),
        out_shape=(jax.ShapeDtypeStruct((rows, 256), jnp.bfloat16),
                   jax.ShapeDtypeStruct((genes // device_count, 256), F32)),
        in_specs=[pl.BlockSpec(memory_space=pl.ANY)] * 2 + [pl.BlockSpec(memory_space=pltpu.VMEM)] * 2,
        out_specs=(pl.BlockSpec(memory_space=pltpu.VMEM),) * 2,
        scratch_shapes=[
            pltpu.VMEM((rows, genes), jnp.bfloat16), pltpu.VMEM((genes, 256), jnp.bfloat16),
            vm(genes, 128), vm(rows, 256), pltpu.VMEM((rows, 256), jnp.bfloat16),
            vm(PLANE, 8, 256), vm(PLANE - 1, 8, 256), vm(8, 256), vm(NZ - 1, 8, 256), vm(8, 256),
            vm(PLANE, 8, 256), vm(256, 256), vm(256, 256), vm(640, 256),
            vm(2, 4, 10, NX, NY, 8, 128), vm(4, 10, NX, NY, 8, 128),
            vm(3, 10, 4, 8, 128), vm(3, 10, 4, 8, 128), vm(3, 10, 4, 8, 128), vm(3, 10, 4, 8, 128),
            vm(2, 10, 4, 8, 128), vm(2, 10, 4, 8, 128),
            vm(3, 10, 8, 128), vm(3, 10, 8, 128), vm(3, 10, 8, 128), vm(3, 10, 8, 128),
            vm(4, 10, 8, 128), vm(NZ, 5, 8, 128), vm(NZ - 1, 5, 8, 128),
            dma((2, CHUNKS)), dma((6,)), dma((2,)), dma((4, 8)), dma((2,)),
        ],
        compiler_params=pltpu.CompilerParams(collective_id=0, has_side_effects=True, vmem_limit_bytes=60 << 20),
    )(counts, gene_basis, gene_scale.reshape(genes // 128, 128), cell_scale.reshape(rows // 128, 128))


def solution(mesh):
    return jax.shard_map(
        local,
        mesh=mesh,
        in_specs=(P(("section", "atlas"), None), P(), P(("section", "atlas")), P()),
        out_specs=(P(("section", "atlas"), None), P(("section", "atlas"), None)),
        check_vma=False,
    )
```

time: 369 us -> 59.5 us (0.16)
  waiting for transfers between devices: 275 us -> 0 us
  other arithmetic: 55.7 us -> 0 us
  Pallas kernels: 0 us -> 55.6 us
  matrix products: 16 us -> 0 us
  between operations: 15.5 us -> 0.64 us
    psum x1 -> x0, waiting for transfers between devices: 275 us -> none  [local(): gram_total = lax.psum(gram_local, ('section', 'atlas'))]
    pallas_call x0 -> x1, Pallas kernels: none -> 55.6 us  [local(): pl.pallas_call(functools.partial(kernel, rows * device_count), out_shape=...]
    another operation x9 -> x0, other arithmetic: 53.9 us -> none  [the longest x6 34.1 us: local(): lower_factor = jnp.linalg.cholesky(gram_total)]
    dot_general x5 -> x0, matrix products: 14.7 us -> none  [the longest x1 5.77 us: local(): jnp.dot(counts, scaled, preferred_element_type=jnp.float32)]
    another operation x9 -> x0, local copies, waits for them, and re-layouts: 4.02 us -> none
  transfers between devices with their start and end apart: 1 -> 0, of which waited for: 1 -> 0; matrix products, arithmetic and copies ran while one was open for 0% -> 0% of each run, Pallas kernels for 0% -> 0%
where the time goes in v1:
time: 59.5 us; the launch traced here: 59.3 us
  Pallas kernels  55.6 us (93%)
  local copies, waits for them, and re-layouts  3.02 us (5%)
  between operations  0.64 us (1%)
    pallas_call x1, Pallas kernels, local(): pl.pallas_call(functools.partial(kernel, rows * device_count), out_shape=...  55.6 us
    unnamed x2, local copies, waits for them, and re-layouts  3.02 us

profile of v1, /device:TPU:1, one launch (start us, length us, event | category | flops | bytes accessed | tf_op | source)
XLA Modules:
  0.0 59.3 jit_solution(7426799777776187542)
XLA Ops:
  0.6 55.6 %shard_map.59 = (bf16[512,256]{1,0:T(8,128)(2,1)}, f32[20,256]{1,0:T(8,128)}) custom-call(bf16[512,5120]{1,0:T(8,128)(2,1)} %counts.1, bf16[5120,256]{1,0:T(8,128)(2,1)} %basis.1, f32[40,128]{1,0:T(8,128)} %bitcast.2, f32[4,128]{1,0:T(4,128)} %bitcast.3), custom_call_target="tpu_custom_call" | custom-call | tf_op jit(solution)/shard_map/pallas_call | solution.py:344
  56.2 1.7 %copy.8 = bf16[512,256]{1,0:T(8,128)(2,1)} copy(bf16[512,256]{1,0:T(8,128)(2,1)} %get-tuple-element.4) | data formatting | bytes 524288
  57.9 1.3 %copy.9 = f32[20,256]{1,0:T(8,128)} copy(f32[20,256]{1,0:T(8,128)} %get-tuple-element.5) | data formatting | bytes 40960

commit v2 on v1

--- a/solution.py
+++ b/solution.py
@@ -48,13 +48,14 @@
         xs = [xs[i] + xs[i + 1] if i + 1 < len(xs) else xs[i] for i in range(0, len(xs), 2)]
     return xs[0]
 
-def invchol128(M):
+def invchol128(M, hook):
     n = len(M)
     M = list(M)
     sub = lax.broadcasted_iota(jnp.int32, (8, 128), 0)
     lane = lax.broadcasted_iota(jnp.int32, (8, 128), 1)
     out = []
     for k in range(n):
+        hook(k)
         blk = (lane >= 8 * k) & (lane < 8 * k + 8)
         Cb = [[jnp.broadcast_to(M[i][:, 8 * k + u:8 * k + u + 1], (8, 128)) for u in range(8)] for i in range(k, n)]
         m = jnp.where(blk, jnp.where(lane == 8 * k + sub, 1.0, 0.0), M[k])
@@ -71,8 +72,8 @@
 def dot(a, b, dims=((1,), (0,))):
     return lax.dot_general(a, b, (dims, ((), ())), precision=HI, preferred_element_type=F32)
 
-def invchol256(g, w, between):
-    o = invchol128([g[8 * i:8 * i + 8, 0:128] for i in range(16)])
+def invchol256(g, w, hook):
+    o = invchol128([g[8 * i:8 * i + 8, 0:128] for i in range(16)], lambda k: hook(0, k))
     for i in range(16):
         w[8 * i:8 * i + 8, 0:128] = o[i]
         w[8 * i:8 * i + 8, 128:256] = jnp.zeros((8, 128), F32)
@@ -80,8 +81,7 @@
     l21 = dot(g[128:256, 0:128], w11, ((1,), (1,)))
     g[128:256, 128:256] = g[128:256, 128:256] - dot(l21, l21, ((1,), (1,)))
     g[128:256, 0:128] = dot(l21, w11)
-    between()
-    o = invchol128([g[128 + 8 * i:136 + 8 * i, 128:256] for i in range(16)])
+    o = invchol128([g[128 + 8 * i:136 + 8 * i, 128:256] for i in range(16)], lambda k: hook(1, k))
     for i in range(16):
         w[128 + 8 * i:136 + 8 * i, 128:256] = o[i]
     w[128:256, 0:128] = -dot(w[128:256, 128:256], g[128:256, 0:128])
@@ -274,6 +274,9 @@
     first.start()
     second.start()
 
+    first.middle()
+    second.middle()
+
     _wait(zr, gsem.at[3])
     gz[...] = gp[...] + jnp.sum(zr[...], axis=0)
     gfull[p] = gz[...]
@@ -284,38 +287,37 @@
             src_ref=gz, dst_ref=gfull.at[p], send_sem=gsem.at[4], recv_sem=gsem.at[5],
             device_id=plane_id(lax.rem(p + d, PLANE)), device_id_type=MESH).start()
 
-    first.middle()
-    second.middle()
-
     _wait(gfull.at[0:PLANE - 1], gsem.at[5])
     g2[...] = gfull[...].reshape(256, 256)
 
     third = Ring4(lambda q, o: PX.at[q, :, o], y, y_id, X2P, X2M, rsem.at[2], Q.at[0:2])
     fourth = Ring4(lambda q, o: PY.at[q, :, o], x, x_id, Y2P, Y2M, rsem.at[3], Q.at[2:4])
 
-    def after_half():
-        first.finish()
-        second.finish()
-        third.start()
-        fourth.start()
-        third.middle()
-        fourth.middle()
-
-    invchol256(g2, w, after_half)
-
-    third.finish()
-    fourth.finish()
-    for k in range(NZ):
-        for t in range(4):
-            zs[k, t] = Q[t, k]
-        zs[k, 4] = Q[k // 2, 8 + k % 2]
-
-    @pl.loop(1, NZ)
-    def _(d):
-        k = lax.rem(z + d, NZ)
-        pltpu.make_async_remote_copy(
-            src_ref=zs.at[k], dst_ref=z3.at[d - 1], send_sem=zsem.at[0], recv_sem=zsem.at[1],
-            device_id=z_id(k), device_id_type=MESH).start()
+    def hook(half, k):
+        if (half, k) == (0, 0):
+            first.finish()
+            second.finish()
+            third.start()
+            fourth.start()
+        elif (half, k) == (0, 8):
+            third.middle()
+            fourth.middle()
+        elif (half, k) == (1, 0):
+            third.finish()
+            fourth.finish()
+            for i in range(NZ):
+                for t in range(4):
+                    zs[i, t] = Q[t, i]
+                zs[i, 4] = Q[i // 2, 8 + i % 2]
+
+            @pl.loop(1, NZ)
+            def _(d):
+                i = lax.rem(z + d, NZ)
+                pltpu.make_async_remote_copy(
+                    src_ref=zs.at[i], dst_ref=z3.at[d - 1], send_sem=zsem.at[0], recv_sem=zsem.at[1],
+                    device_id=z_id(i), device_id_type=MESH).start()
+
+    invchol256(g2, w, hook)
 
     cell_basis[...] = dot(sk[...], w[...], ((1,), (1,))).astype(jnp.bfloat16)
 
@@ -336,15 +338,21 @@
     _wait(z3, zsem.at[0])
 
 
+def hand_on(a, b, a_out, b_out):
+    a_out[...] = a[...]
+    b_out[...] = b[...]
+
+
 def local(counts, gene_scale, cell_scale, gene_basis):
     device_count = lax.axis_size("section") * lax.axis_size("atlas")
     rows, genes = counts.shape
     vm = lambda *s: pltpu.VMEM(s, F32)
     dma = pltpu.SemaphoreType.DMA
-    return pl.pallas_call(
+    shapes = (jax.ShapeDtypeStruct((rows, 256), jnp.bfloat16),
+              jax.ShapeDtypeStruct((genes // device_count, 256), F32))
+    result = pl.pallas_call(
         functools.partial(kernel, rows * device_count),
-        out_shape=(jax.ShapeDtypeStruct((rows, 256), jnp.bfloat16),
-                   jax.ShapeDtypeStruct((genes // device_count, 256), F32)),
+        out_shape=shapes,
         in_specs=[pl.BlockSpec(memory_space=pl.ANY)] * 2 + [pl.BlockSpec(memory_space=pltpu.VMEM)] * 2,
         out_specs=(pl.BlockSpec(memory_space=pltpu.VMEM),) * 2,
         scratch_shapes=[
@@ -361,6 +369,7 @@
         ],
         compiler_params=pltpu.CompilerParams(collective_id=0, has_side_effects=True, vmem_limit_bytes=60 << 20),
     )(counts, gene_basis, gene_scale.reshape(genes // 128, 128), cell_scale.reshape(rows // 128, 128))
+    return pl.pallas_call(hand_on, out_shape=shapes)(*result)
 
 
 def solution(mesh):

time: 59.5 us -> 57 us (0.958)
  local copies, waits for them, and re-layouts: 3.02 us -> 0 us
    unnamed x2 -> x0, local copies, waits for them, and re-layouts: 3.02 us -> none
    pallas_call x0 -> x1, Pallas kernels: none -> 1.68 us  [local(): return pl.pallas_call(hand_on, out_shape=shapes)(*result)]
    pallas_call x1, Pallas kernels: 55.6 us -> 54.3 us  [local(): pl.pallas_call(functools.partial(kernel, rows * device_count), out_shape=...]
where the time goes in v2:
time: 57 us; the launch traced here: 56.7 us
  Pallas kernels  56 us (98%)
  between operations  0.64 us (1%)
    pallas_call x1, Pallas kernels, local(): pl.pallas_call(functools.partial(kernel, rows * device_count), out_shape=...  54.3 us
    pallas_call x1, Pallas kernels, local(): return pl.pallas_call(hand_on, out_shape=shapes)(*result)  1.68 us

profile of v2, /device:TPU:1, one launch (start us, length us, event | category | flops | bytes accessed | tf_op | source)
XLA Modules:
  0.0 56.7 jit_solution(12449962539604400733)
XLA Ops:
  0.6 54.3 %shard_map.59 = (bf16[512,256]{1,0:T(8,128)(2,1)}, f32[20,256]{1,0:T(8,128)}) custom-call(bf16[512,5120]{1,0:T(8,128)(2,1)} %counts.1, bf16[5120,256]{1,0:T(8,128)(2,1)} %basis.1, f32[40,128]{1,0:T(8,128)} %bitcast.2, f32[4,128]{1,0:T(4,128)} %bitcast.3), custom_call_target="tpu_custom_call" | custom-call | tf_op jit(solution)/shard_map/pallas_call | solution.py:353
  55.0 1.7 %shard_map.60 = (bf16[512,256]{1,0:T(8,128)(2,1)}, f32[20,256]{1,0:T(8,128)}) custom-call(bf16[512,256]{1,0:T(8,128)(2,1)} %get-tuple-element.4.a, f32[20,256]{1,0:T(8,128)} %get-tuple-element.5.b), custom_call_target="tpu_custom_call" | custom-call | tf_op jit(solution)/shard_map/pallas_call | solution.py:372

commit v3 on v2

v3 whole, which is shorter than its diff:
```python
import functools

import jax
import jax.numpy as jnp
from jax import lax
from jax.experimental import pallas as pl
from jax.experimental.pallas import tpu as pltpu
from jax.sharding import PartitionSpec as P

HI = lax.Precision.HIGHEST
F32 = jnp.float32

def _sub(x, j):
    return jnp.broadcast_to(x[j:j + 1, :], x.shape)

def sweep(C, sub):
    C = list(C)
    Wt = [jnp.zeros((8, 128), F32) for _ in range(8)]
    piv = jnp.ones((8, 128), F32)
    for j in range(0, 8, 2):
        a, b, c = _sub(C[j], j), _sub(C[j], j + 1), _sub(C[j + 1], j + 1)
        r = 1.0 / (a * c - b * b)
        i11, i12, i22 = c * r, -b * r, a * r
        ra = 1.0 / a
        e = b * ra
        piv = jnp.where(sub == j, a, jnp.where(sub == j + 1, c - b * e, piv))
        for k in range(j):
            low = C[k] - e * _sub(C[k], j)
            Wt[k] = jnp.where(sub == j, C[k], jnp.where(sub == j + 1, low, Wt[k]))
        Wt[j] = jnp.where(sub == j, 1.0, jnp.where(sub == j + 1, -e, Wt[j]))
        Wt[j + 1] = jnp.where(sub == j + 1, 1.0, Wt[j + 1])
        for k in range(8):
            if k not in (j, j + 1):
                q0, q1 = _sub(C[k], j), _sub(C[k], j + 1)
                s0 = i11 * q0 + i12 * q1
                s1 = i12 * q0 + i22 * q1
                new = C[k] - (C[j] * s0 + C[j + 1] * s1)
                C[k] = jnp.where(sub == j, s0, jnp.where(sub == j + 1, s1, new))
        x, y = C[j], C[j + 1]
        C[j] = jnp.where(sub == j, i11, jnp.where(sub == j + 1, i12, -(x * i11 + y * i12)))
        C[j + 1] = jnp.where(sub == j, i12, jnp.where(sub == j + 1, i22, -(x * i12 + y * i22)))
    rs = lax.rsqrt(piv)
    return C, [w * rs for w in Wt]

def tree(xs):
    xs = list(xs)
    while len(xs) > 1:
        xs = [xs[i] + xs[i + 1] if i + 1 < len(xs) else xs[i] for i in range(0, len(xs), 2)]
    return xs[0]

def invchol128(M, hook):
    n = len(M)
    M = list(M)
    sub = lax.broadcasted_iota(jnp.int32, (8, 128), 0)
    lane = lax.broadcasted_iota(jnp.int32, (8, 128), 1)
    out = []
    for k in range(n):
        hook(k)
        blk = (lane >= 8 * k) & (lane < 8 * k + 8)
        Cb = [[jnp.broadcast_to(M[i][:, 8 * k + u:8 * k + u + 1], (8, 128)) for u in range(8)] for i in range(k, n)]
        m = jnp.where(blk, jnp.where(lane == 8 * k + sub, 1.0, 0.0), M[k])
        mb = [_sub(m, u) for u in range(8)]
        P, W8 = sweep(Cb[0], sub)
        T = tree([P[u] * mb[u] for u in range(8)])
        Tb = [_sub(T, u) for u in range(8)]
        for i in range(k + 1, n):
            M[i] = jnp.where(blk, 0.0, M[i]) - tree([Cb[i - k][u] * Tb[u] for u in range(8)])
        row = tree([W8[u] * mb[u] for u in range(8)])
        out.append(jnp.where(lane < 8 * k + 8, row, 0.0))
    return out

def dot(a, b, dims=((1,), (0,))):
    return lax.dot_general(a, b, (dims, ((), ())), precision=HI, preferred_element_type=F32)

def rows_of(tiles, part):
    return jnp.concatenate([tiles[i, part] for i in range(16)], axis=0)


def inverse_factor(tiles, w, tmp, hook):
    o = invchol128([tiles[i, 0] for i in range(16)], lambda k: hook(0, k))
    for i in range(16):
        w[8 * i:8 * i + 8, 0:128] = o[i]
        w[8 * i:8 * i + 8, 128:256] = jnp.zeros((8, 128), F32)
    w11 = w[0:128, 0:128]
    l21 = dot(rows_of(tiles, 1), w11, ((1,), (1,)))
    s = rows_of(tiles, 2) - dot(l21, l21, ((1,), (1,)))
    tmp[...] = dot(l21, w11)
    o = invchol128([s[8 * i:8 * i + 8] for i in range(16)], lambda k: hook(1, k))
    for i in range(16):
        w[128 + 8 * i:136 + 8 * i, 128:256] = o[i]
    w[128:256, 0:128] = -dot(w[128:256, 128:256], tmp[...])


MESH = pl.DeviceIdType.MESH
NZ, NX, NY = 8, 4, 4
PLANE = NX * NY * 2
CUTS = (0, 1536, 3072, 4352, 5120)
CHUNKS = len(CUTS) - 1


def _wait(view, sem):
    pltpu.make_async_copy(view, view, sem).wait()


def _column(rows):
    r = rows.shape[0]
    return jnp.concatenate([rows, jnp.zeros((128 - r, 128), F32)], axis=0).T


class Ring4:
    def __init__(self, block, i, ids, plus, minus, sems, out):
        self.block, self.plus, self.minus, self.sems, self.out = block, plus, minus, sems, out
        self.i, self.ids = i, ids
        self.up, self.down, self.far = lax.rem(i + 1, 4), lax.rem(i + 3, 4), lax.rem(i + 2, 4)

    def send(self, q, owner, forward, slot):
        buf = self.plus if forward else self.minus
        pltpu.make_async_remote_copy(
            src_ref=self.block(q, owner),
            dst_ref=buf.at[slot],
            send_sem=self.sems.at[6 if forward else 7],
            recv_sem=self.sems.at[slot if forward else 3 + slot],
            device_id=self.ids(self.up if forward else self.down),
            device_id_type=MESH,
        ).start()

    def start(self):
        self.send(0, self.far, True, 0)
        self.send(1, self.far, False, 0)

    def middle(self):
        _wait(self.plus.at[0], self.sems.at[0])
        ref = self.block(0, self.up)
        ref[...] = ref[...] + self.plus[0]
        self.send(0, self.up, True, 2)
        _wait(self.minus.at[0], self.sems.at[3])
        ref = self.block(1, self.down)
        ref[...] = ref[...] + self.minus[0]
        self.send(1, self.down, False, 2)
        self.send(1, self.up, True, 1)
        self.send(0, self.down, False, 1)

    def finish(self):
        for s in (1, 2):
            _wait(self.plus.at[s], self.sems.at[s])
            _wait(self.minus.at[s], self.sems.at[3 + s])
        self.out[0] = self.block(0, self.i)[...] + (self.plus[2] + self.minus[1])
        self.out[1] = self.block(1, self.i)[...] + (self.plus[1] + self.minus[2])

    def drain(self):
        _wait(self.plus, self.sems.at[6])
        _wait(self.minus, self.sems.at[7])


class Ring8:
    def __init__(self, data, z, ids, plus, minus, sems):
        self.data, self.z, self.plus, self.minus, self.sems = data, z, plus, minus, sems
        self.next, self.last = ids(lax.rem(z + 1, 8)), ids(lax.rem(z + 7, 8))

    def send(self, step, src_up, src_down):
        lo, hi = (0, 2) if step == 0 else (4 * step - 2, 4 * step + 2)
        for src, buf, device, side in ((src_up, self.plus, self.next, 0), (src_down, self.minus, self.last, 1)):
            pltpu.make_async_remote_copy(
                src_ref=src, dst_ref=buf.at[lo:hi], send_sem=self.sems.at[8 + side],
                recv_sem=self.sems.at[4 * side + step], device_id=device, device_id_type=MESH).start()

    def start(self):
        far = lax.rem(self.z + 4, 8)
        self.send(0, self.data.at[far, 0:2], self.data.at[far, 2:4])

    def step(self, k):
        lo, hi = (0, 2) if k == 1 else (4 * k - 6, 4 * k - 2)
        up, down = lax.rem(self.z + 4 - k, 8), lax.rem(self.z + 4 + k, 8)
        for buf, at, part, side in ((self.plus, up, slice(0, 2), 0), (self.minus, down, slice(2, 4), 1)):
            _wait(buf.at[lo:hi], self.sems.at[4 * side + k - 1])
            ref = self.data.at[at, part] if k == 1 else self.data.at[at]
            ref[...] = ref[...] + buf[lo:hi]
        self.send(k, self.data.at[up], self.data.at[down])

    def finish(self, out):
        for side, buf in enumerate((self.plus, self.minus)):
            _wait(buf.at[10:14], self.sems.at[4 * side + 3])
        out[...] = self.data[self.z] + (self.plus[10:14] + self.minus[10:14])

    def drain(self):
        _wait(self.plus, self.sems.at[8])
        _wait(self.minus, self.sems.at[9])


def kernel(cells_all, counts, basis, scale, cells, cell_basis, gene_side,
           cbuf, bbuf, sbc, sk, wt, gl, gr, gp, zr, gz, gfull, w, tmp, stg, S, R, SZ, RZ, ZP, ZM, zt, zq,
           XP, XM, YP, YM, PX, PY, X2P, X2M, Y2P, Y2M, Q, zs, z3,
           load_sem, gsem, csem, rsem, zsem, qsem):
    sec = lax.axis_index("section")
    y = lax.axis_index("atlas")
    c = lax.rem(sec, 2)
    x = lax.rem(sec // 2, NX)
    z = sec // (2 * NX)
    h = x * NY + y

    def z_id(k):
        return ((k * NX + x) * 2 + c, y)

    def x_id(k):
        return ((z * NX + k) * 2 + c, y)

    def y_id(k):
        return (sec, k)

    partner = (sec + 1 - 2 * c, y)
    others = []
    for dx in (2, 1, 3, 0):
        for dy in (2, 1, 3, 0):
            if dx or dy:
                px, py = lax.rem(x + dx, NX), lax.rem(y + dy, NY)
                others.append((dx * NY + dy, px * NY + py, [((z * NX + px) * 2 + b, py) for b in range(2)]))

    def put(src, dst, pair, device):
        pltpu.make_async_remote_copy(
            src_ref=src, dst_ref=dst, send_sem=pair.at[0], recv_sem=pair.at[1],
            device_id=device, device_id_type=MESH).start()

    def by_core(fn):
        for b in range(2):
            pl.when(c == b)(functools.partial(fn, b))

    def loads(k):
        cols = slice(CUTS[k], CUTS[k + 1])
        return (pltpu.make_async_copy(counts.at[:, cols], cbuf.at[:, cols], load_sem.at[0, k]),
                pltpu.make_async_copy(basis.at[cols, :], bbuf.at[cols, :], load_sem.at[1, k]))

    for k in range(CHUNKS):
        for copy in loads(k):
            copy.start()

    barrier = pltpu.get_barrier_semaphore()
    for _, _, ids in others:
        for device in ids:
            pl.semaphore_signal(barrier, inc=1, device_id=device, device_id_type=MESH)
    pl.semaphore_signal(barrier, inc=1, device_id=partner, device_id_type=MESH)

    @pl.loop(1, NZ)
    def _(d):
        pl.semaphore_signal(barrier, inc=1, device_id=z_id(lax.rem(z + d, NZ)), device_id_type=MESH)

    turned = _column(scale[...])
    for g in range(scale.shape[0]):
        sbc[128 * g:128 * g + 128, :] = jnp.broadcast_to(turned[:, g:g + 1], (128, 128))
    for k in range(CHUNKS):
        for copy in loads(k):
            copy.wait()
        rows = slice(CUTS[k], CUTS[k + 1])
        factor = sbc[rows, :]
        part = bbuf[rows, :].astype(F32)
        scaled = jnp.concatenate([part[:, :128] * factor, part[:, 128:] * factor], axis=1).astype(jnp.bfloat16)
        term = jnp.dot(cbuf[:, rows], scaled, preferred_element_type=F32)
        sk[...] = term if k == 0 else sk[...] + term

    turned = _column(cells[...])
    for r in range(cells.shape[0]):
        rows = slice(128 * r, 128 * r + 128)
        factor = jnp.broadcast_to(turned[:, r:r + 1], (128, 256))
        value = sk[rows, :] * factor
        sk[rows, :] = value
        wt[rows, :] = (value * factor).astype(jnp.bfloat16)

    gram = dot(sk[...], sk[...], ((0,), (0,))) * (1.0 / cells_all)
    for i in range(16):
        gl[i, 0] = gram[8 * i:8 * i + 8, :128]
        gl[i, 1] = gram[128 + 8 * i:136 + 8 * i, :128]
        gl[i, 2] = gram[128 + 8 * i:136 + 8 * i, 128:]

    pl.semaphore_wait(barrier, PLANE - 1 + NZ - 1)

    for r, chip, ids in others:
        place = (2 * r + c) * 2
        put(gl.at[chip, 0:1], gr.at[pl.ds(place, 1)], gsem.at[0], ids[0])
        put(gl.at[chip, 1:3], gr.at[pl.ds(place, 2)], gsem.at[0], ids[1])

    def to_partner(b):
        n = 2 - b
        put(gl.at[h, 1 - b:1 - b + n], gr.at[2 * b:2 * b + n], gsem.at[0], partner)
        gr[2 * b] = gl[h, b]
        gr[2 * b + 1] = gl[h, 2 * b]

    by_core(to_partner)

    def sums(batch, begin, end):
        @pl.loop(begin, end)
        def _(j):
            cols = pl.ds(pl.multiple_of((2 * j + batch) * 640, 128), 640)
            part = lax.dot_general(cbuf[:, cols], wt[...], (((0,), (0,)), ((), ())), preferred_element_type=F32)
            factor = sbc[cols, :] * (1.0 / cells_all)
            stg[:, :128] = part[:, :128] * factor
            stg[:, 128:] = part[:, 128:] * factor
            for a in range(NX):
                for b in range(2):
                    for e in range(NY):
                        o = ((a * 2 + b) * NY + e) * 20
                        S[b, batch, 0, j, a, e] = stg[o:o + 8, :128]
                        S[b, batch, 1, j, a, e] = stg[o:o + 8, 128:]
                        S[b, batch, 2, j, a, e] = stg[o + 8:o + 16, :128]
                        S[b, batch, 3, j, a, e] = stg[o + 8:o + 16, 128:]
                        SZ[b, 2 * j + batch, a, e] = jnp.concatenate(
                            [stg[o + 16:o + 20, :128], stg[o + 16:o + 20, 128:]], axis=0)
            put(S.at[1 - c, batch, :, j], R.at[batch, :, j], csem.at[batch], partner)
            put(SZ.at[1 - c, 2 * j + batch], RZ.at[2 * j + batch], csem.at[2], partner)

    sums(0, 0, 4)
    sums(1, 0, 2)

    first, second, third, fourth = [], [], [], []
    for batch in range(2):
        first.append(Ring4(lambda q, o, n=batch: R.at[n, q, :, o], x, x_id,
                           XP.at[batch], XM.at[batch], rsem.at[batch, 0], PX.at[batch]))
        second.append(Ring4(lambda q, o, n=batch: R.at[n, 2 + q, :, :, o], y, y_id,
                            YP.at[batch], YM.at[batch], rsem.at[batch, 1], PY.at[batch]))
        third.append(Ring4(lambda q, o, n=batch: PX.at[n, q, :, o], y, y_id,
                           X2P.at[batch], X2M.at[batch], rsem.at[batch, 2], Q.at[batch, 0:2]))
        fourth.append(Ring4(lambda q, o, n=batch: PY.at[n, q, :, o], x, x_id,
                            Y2P.at[batch], Y2M.at[batch], rsem.at[batch, 3], Q.at[batch, 2:4]))

    def add_partner(batch):
        _wait(R.at[batch], csem.at[batch, 1])

        @pl.loop(0, 4)
        def _(u):
            for q in range(4):
                R[batch, q, u] = R[batch, q, u] + S[c, batch, q, u]

    def stage_one(batch):
        first[batch].start()
        second[batch].start()

    def stage_one_middle(batch):
        first[batch].middle()
        second[batch].middle()

    def stage_two(batch):
        first[batch].finish()
        third[batch].start()
        second[batch].finish()
        fourth[batch].start()

    def stage_two_middle(batch):
        third[batch].middle()
        fourth[batch].middle()

    def stage_three(batch):
        third[batch].finish()
        fourth[batch].finish()
        for j in range(NZ // 2):
            k = 2 * j + batch
            for t in range(4):
                zs[k, t] = Q[batch, t, j]
            d = lax.rem(k - z + NZ, NZ)

            @pl.when(d > 0)
            def _():
                put(zs.at[k], z3.at[d - 1], zsem, z_id(k))

    over = Ring8(RZ, z, z_id, ZP, ZM, qsem)

    def z_start():
        _wait(RZ, csem.at[2, 1])

        @pl.loop(0, NZ)
        def _(k):
            RZ[k] = RZ[k] + SZ[c, k]

        over.start()

    def z_finish():
        over.finish(zt)
        zq[0] = zt[x, y]
        for r, chip, ids in others:
            pltpu.make_async_remote_copy(
                src_ref=zt.at[chip // NY, lax.rem(chip, NY)], dst_ref=zq.at[r], send_sem=qsem.at[10], recv_sem=qsem.at[11],
                device_id=(ids[0][0] + c, ids[0][1]), device_id_type=MESH).start()

    add_partner(0)
    stage_one(0)
    sums(1, 2, 4)

    by_core(lambda b: _wait(gr.at[0:31 * (b + 1)], gsem.at[0, 1]))
    gp[...] = jnp.sum(gr[...].reshape(PLANE, 2, 8, 128), axis=0)

    def over_z(b):
        @pl.loop(1, NZ)
        def _(d):
            put(gp.at[0:b + 1], zr.at[pl.ds(2 * (d - 1), b + 1)], gsem.at[1], z_id(lax.rem(z + d, NZ)))

    by_core(over_z)

    add_partner(1)
    z_start()

    stage_one_middle(0)

    by_core(lambda b: _wait(zr.at[0:7 * (b + 1)], gsem.at[1, 1]))
    gz[...] = gp[...] + jnp.sum(zr[...].reshape(NZ - 1, 2, 8, 128), axis=0)

    def spread(b):
        n = b + 1
        gfull[h, b] = gz[0]
        if b:
            gfull[h, 2] = gz[1]
        for _, _, ids in others:
            put(gz.at[0:n], gfull.at[h, b:b + n], gsem.at[2], ids[b])

    by_core(spread)

    stage_one(1)
    over.step(1)

    def hand_over(b):
        n = b + 1
        _wait(gr.at[0:15 * n], gsem.at[2, 1])
        put(gfull.at[:, b:b + n], gfull.at[:, b:b + n], gsem.at[3], partner)

    by_core(hand_over)
    stage_two(0)
    over.step(2)
    stage_one_middle(1)
    by_core(lambda b: _wait(gr.at[0:16 * (2 - b)], gsem.at[3, 1]))

    events = {
        (0, 2): lambda: over.step(3),
        (0, 4): lambda: stage_two_middle(0),
        (0, 10): lambda: stage_three(0),
        (0, 13): z_finish,
        (0, 15): lambda: stage_two(1),
        (1, 2): lambda: stage_two_middle(1),
        (1, 9): lambda: stage_three(1),
    }

    def hook(half, k):
        if (half, k) in events:
            with jax.named_scope(f"e{half}_{k}"):
                events[half, k]()

    inverse_factor(gfull, w, tmp, hook)

    cell_basis[...] = dot(sk[...], w[...], ((1,), (1,))).astype(jnp.bfloat16)

    _wait(z3, zsem.at[1])
    _wait(zq.at[1:16], qsem.at[11])
    own = zs[z] + jnp.sum(z3[...], axis=0)
    top = jnp.concatenate([own[0], own[1]], axis=1)
    mid = jnp.concatenate([own[2], own[3]], axis=1)
    rest = jnp.sum(zq[...], axis=0)
    low = jnp.concatenate([rest, pltpu.roll(rest, 4, 0)], axis=1)
    side = dot(jnp.concatenate([top, mid, low], axis=0), w[...], ((1,), (1,)))
    gene_side[...] = side[:20]

    def drain(b):
        _wait(gr.at[0:47 - b], gsem.at[0, 0])
        _wait(zr.at[0:7 * (b + 1)], gsem.at[1, 0])
        _wait(gr.at[0:15 * (b + 1)], gsem.at[2, 0])
        _wait(gr.at[0:16 * (b + 1)], gsem.at[3, 0])

    by_core(drain)
    for batch in range(2):
        _wait(R.at[batch], csem.at[batch, 0])
        for ring in (first[batch], second[batch], third[batch], fourth[batch]):
            ring.drain()
    _wait(z3, zsem.at[0])
    _wait(RZ, csem.at[2, 0])
    over.drain()
    _wait(zq.at[1:16], qsem.at[10])


def hand_on(a, b, a_out, b_out):
    a_out[...] = a[...]
    b_out[...] = b[...]


def local(counts, gene_scale, cell_scale, gene_basis):
    device_count = lax.axis_size("section") * lax.axis_size("atlas")
    rows, genes = counts.shape
    vm = lambda *s: pltpu.VMEM(s, F32)
    dma = pltpu.SemaphoreType.DMA
    shapes = (jax.ShapeDtypeStruct((rows, 256), jnp.bfloat16),
              jax.ShapeDtypeStruct((genes // device_count, 256), F32))
    result = pl.pallas_call(
        functools.partial(kernel, rows * device_count),
        out_shape=shapes,
        in_specs=[pl.BlockSpec(memory_space=pl.ANY)] * 2 + [pl.BlockSpec(memory_space=pltpu.VMEM)] * 2,
        out_specs=(pl.BlockSpec(memory_space=pltpu.VMEM),) * 2,
        scratch_shapes=[
            pltpu.VMEM((rows, genes), jnp.bfloat16), pltpu.VMEM((genes, 256), jnp.bfloat16),
            vm(genes, 128), vm(rows, 256), pltpu.VMEM((rows, 256), jnp.bfloat16),
            vm(16, 3, 8, 128), vm(64, 8, 128), vm(2, 8, 128), vm(14, 8, 128), vm(2, 8, 128),
            vm(16, 3, 8, 128), vm(256, 256), vm(128, 128), vm(640, 256),
            vm(2, 2, 4, 4, NX, NY, 8, 128), vm(2, 4, 4, NX, NY, 8, 128),
            vm(2, NZ, NX, NY, 8, 128), vm(NZ, NX, NY, 8, 128), vm(14, NY, 8, 128), vm(14, NY, 8, 128),
            vm(NX, NY, 8, 128), vm(NX * NY, 8, 128),
            vm(2, 3, 4, 4, 8, 128), vm(2, 3, 4, 4, 8, 128), vm(2, 3, 4, 4, 8, 128), vm(2, 3, 4, 4, 8, 128),
            vm(2, 2, 4, 4, 8, 128), vm(2, 2, 4, 4, 8, 128),
            vm(2, 3, 4, 8, 128), vm(2, 3, 4, 8, 128), vm(2, 3, 4, 8, 128), vm(2, 3, 4, 8, 128),
            vm(2, 4, 4, 8, 128), vm(NZ, 4, 8, 128), vm(NZ - 1, 4, 8, 128),
            dma((2, CHUNKS)), dma((4, 2)), dma((3, 2)), dma((2, 4, 8)), dma((2,)), dma((12,)),
        ],
        compiler_params=pltpu.CompilerParams(collective_id=0, has_side_effects=True, vmem_limit_bytes=60 << 20),
    )(counts, gene_basis, gene_scale.reshape(genes // 128, 128), cell_scale.reshape(rows // 128, 128))
    return pl.pallas_call(hand_on, out_shape=shapes)(*result)


def solution(mesh):
    return jax.shard_map(
        local,
        mesh=mesh,
        in_specs=(P(("section", "atlas"), None), P(), P(("section", "atlas")), P()),
        out_specs=(P(("section", "atlas"), None), P(("section", "atlas"), None)),
        check_vma=False,
    )
```

time: 57 us -> 56.3 us (0.988)
  the two profiles are of different devices: /device:TPU:1 before, /device:TPU:32 now
where the time goes in v3:
time: 56.3 us; the launch traced here: 56.1 us
  Pallas kernels  55.5 us (99%)
  between operations  0.64 us (1%)
    pallas_call x1, Pallas kernels, local(): pl.pallas_call(functools.partial(kernel, rows * device_count), out_shape=...  53.8 us
    pallas_call x1, Pallas kernels, local(): return pl.pallas_call(hand_on, out_shape=shapes)(*result)  1.68 us

profile of v3, /device:TPU:32, one launch (start us, length us, event | category | flops | bytes accessed | tf_op | source)
XLA Modules:
  0.0 56.1 jit_solution(17072169801701306555)
XLA Ops:
  0.6 53.8 %shard_map.59 = (bf16[512,256]{1,0:T(8,128)(2,1)}, f32[20,256]{1,0:T(8,128)}) custom-call(bf16[512,5120]{1,0:T(8,128)(2,1)} %counts.1, bf16[5120,256]{1,0:T(8,128)(2,1)} %basis.1, f32[40,128]{1,0:T(8,128)} %bitcast.2, f32[4,128]{1,0:T(4,128)} %bitcast.3), custom_call_target="tpu_custom_call" | custom-call | tf_op jit(solution)/shard_map/pallas_call | solution.py:485
  54.4 1.7 %shard_map.60 = (bf16[512,256]{1,0:T(8,128)(2,1)}, f32[20,256]{1,0:T(8,128)}) custom-call(bf16[512,256]{1,0:T(8,128)(2,1)} %get-tuple-element.4.a, f32[20,256]{1,0:T(8,128)} %get-tuple-element.5.b), custom_call_target="tpu_custom_call" | custom-call | tf_op jit(solution)/shard_map/pallas_call | solution.py:506

commit v4 on v3

--- a/solution.py
+++ b/solution.py
@@ -224,14 +224,19 @@
         for b in range(2):
             pl.when(c == b)(functools.partial(fn, b))
 
+    def alone(fn):
+        pl.when(sec >= 0)(fn)
+
     def loads(k):
         cols = slice(CUTS[k], CUTS[k + 1])
         return (pltpu.make_async_copy(counts.at[:, cols], cbuf.at[:, cols], load_sem.at[0, k]),
                 pltpu.make_async_copy(basis.at[cols, :], bbuf.at[cols, :], load_sem.at[1, k]))
 
-    for k in range(CHUNKS):
-        for copy in loads(k):
-            copy.start()
+    @alone
+    def _():
+        for k in range(CHUNKS):
+            for copy in loads(k):
+                copy.start()
 
     barrier = pltpu.get_barrier_semaphore()
     for _, _, ids in others:
@@ -379,7 +384,7 @@
                 device_id=(ids[0][0] + c, ids[0][1]), device_id_type=MESH).start()
 
     add_partner(0)
-    stage_one(0)
+    alone(lambda: stage_one(0))
     sums(1, 2, 4)
 
     by_core(lambda b: _wait(gr.at[0:31 * (b + 1)], gsem.at[0, 1]))
@@ -393,9 +398,10 @@
     by_core(over_z)
 
     add_partner(1)
-    z_start()
-
-    stage_one_middle(0)
+    alone(z_start)
+    alone(lambda: stage_one(1))
+
+    alone(lambda: stage_one_middle(0))
 
     by_core(lambda b: _wait(zr.at[0:7 * (b + 1)], gsem.at[1, 1]))
     gz[...] = gp[...] + jnp.sum(zr[...].reshape(NZ - 1, 2, 8, 128), axis=0)
@@ -410,8 +416,10 @@
 
     by_core(spread)
 
-    stage_one(1)
-    over.step(1)
+    alone(lambda: over.step(1))
+    alone(lambda: stage_one_middle(1))
+    alone(lambda: stage_two(0))
+    alone(lambda: over.step(2))
 
     def hand_over(b):
         n = b + 1
@@ -419,25 +427,22 @@
         put(gfull.at[:, b:b + n], gfull.at[:, b:b + n], gsem.at[3], partner)
 
     by_core(hand_over)
-    stage_two(0)
-    over.step(2)
-    stage_one_middle(1)
     by_core(lambda b: _wait(gr.at[0:16 * (2 - b)], gsem.at[3, 1]))
 
     events = {
-        (0, 2): lambda: over.step(3),
-        (0, 4): lambda: stage_two_middle(0),
-        (0, 10): lambda: stage_three(0),
-        (0, 13): z_finish,
-        (0, 15): lambda: stage_two(1),
-        (1, 2): lambda: stage_two_middle(1),
-        (1, 9): lambda: stage_three(1),
+        (0, 2): lambda: stage_two(1),
+        (0, 5): lambda: stage_two_middle(0),
+        (0, 8): lambda: over.step(3),
+        (0, 11): lambda: stage_two_middle(1),
+        (0, 14): lambda: stage_three(0),
+        (1, 2): z_finish,
+        (1, 5): lambda: stage_three(1),
     }
 
     def hook(half, k):
         if (half, k) in events:
             with jax.named_scope(f"e{half}_{k}"):
-                events[half, k]()
+                alone(events[half, k])
 
     inverse_factor(gfull, w, tmp, hook)
 

time: 56.3 us -> 46.6 us (0.83)
  the two profiles are of different devices: /device:TPU:32 before, /device:TPU:1 now
where the time goes in v4:
time: 46.6 us; the launch traced here: 46.5 us
  Pallas kernels  45.8 us (98%)
  between operations  0.64 us (1%)
    pallas_call x1, Pallas kernels, local(): pl.pallas_call(functools.partial(kernel, rows * device_count), out_shape=...  44.1 us
    pallas_call x1, Pallas kernels, local(): return pl.pallas_call(hand_on, out_shape=shapes)(*result)  1.68 us

profile of v4, /device:TPU:1, one launch (start us, length us, event | category | flops | bytes accessed | tf_op | source)
XLA Modules:
  0.0 46.5 jit_solution(13631821122805266507)
XLA Ops:
  0.6 44.1 %shard_map.59 = (bf16[512,256]{1,0:T(8,128)(2,1)}, f32[20,256]{1,0:T(8,128)}) custom-call(bf16[512,5120]{1,0:T(8,128)(2,1)} %counts.1, bf16[5120,256]{1,0:T(8,128)(2,1)} %basis.1, f32[40,128]{1,0:T(8,128)} %bitcast.2, f32[4,128]{1,0:T(4,128)} %bitcast.3), custom_call_target="tpu_custom_call" | custom-call | tf_op jit(solution)/shard_map/pallas_call | solution.py:490
  44.8 1.7 %shard_map.60 = (bf16[512,256]{1,0:T(8,128)(2,1)}, f32[20,256]{1,0:T(8,128)}) custom-call(bf16[512,256]{1,0:T(8,128)(2,1)} %get-tuple-element.4.a, f32[20,256]{1,0:T(8,128)} %get-tuple-element.5.b), custom_call_target="tpu_custom_call" | custom-call | tf_op jit(solution)/shard_map/pallas_call | solution.py:511

commit v5 on v4

--- a/solution.py
+++ b/solution.py
@@ -57,14 +57,19 @@
     for k in range(n):
         hook(k)
         blk = (lane >= 8 * k) & (lane < 8 * k + 8)
-        Cb = [[jnp.broadcast_to(M[i][:, 8 * k + u:8 * k + u + 1], (8, 128)) for u in range(8)] for i in range(k, n)]
+        Cb = [[jnp.broadcast_to(M[i][:, 8 * k + u:8 * k + u + 1], (8, 128)) for u in range(8)]
+              for i in range(k, min(k + 2, n))]
         m = jnp.where(blk, jnp.where(lane == 8 * k + sub, 1.0, 0.0), M[k])
         mb = [_sub(m, u) for u in range(8)]
-        P, W8 = sweep(Cb[0], sub)
+        P, W8 = sweep([jnp.where(lane < 128, v, 0.0) for v in Cb[0]], sub)
         T = tree([P[u] * mb[u] for u in range(8)])
         Tb = [_sub(T, u) for u in range(8)]
-        for i in range(k + 1, n):
-            M[i] = jnp.where(blk, 0.0, M[i]) - tree([Cb[i - k][u] * Tb[u] for u in range(8)])
+        if k + 1 < n:
+            M[k + 1] = jnp.where(blk, 0.0, M[k + 1]) - tree([Cb[1][u] * Tb[u] for u in range(8)])
+        if k + 2 < n:
+            update = dot(jnp.concatenate(M[k + 2:], axis=0)[:, 8 * k:8 * k + 8], T)
+            for i in range(k + 2, n):
+                M[i] = jnp.where(blk, 0.0, M[i]) - update[8 * (i - k - 2):8 * (i - k - 1)]
         row = tree([W8[u] * mb[u] for u in range(8)])
         out.append(jnp.where(lane < 8 * k + 8, row, 0.0))
     return out
@@ -293,7 +298,7 @@
     def sums(batch, begin, end):
         @pl.loop(begin, end)
         def _(j):
-            cols = pl.ds(pl.multiple_of((2 * j + batch) * 640, 128), 640)
+            cols = pl.ds(pl.multiple_of((4 * batch + j) * 640, 128), 640)
             part = lax.dot_general(cbuf[:, cols], wt[...], (((0,), (0,)), ((), ())), preferred_element_type=F32)
             factor = sbc[cols, :] * (1.0 / cells_all)
             stg[:, :128] = part[:, :128] * factor
@@ -306,10 +311,10 @@
                         S[b, batch, 1, j, a, e] = stg[o:o + 8, 128:]
                         S[b, batch, 2, j, a, e] = stg[o + 8:o + 16, :128]
                         S[b, batch, 3, j, a, e] = stg[o + 8:o + 16, 128:]
-                        SZ[b, 2 * j + batch, a, e] = jnp.concatenate(
+                        SZ[b, 4 * batch + j, a, e] = jnp.concatenate(
                             [stg[o + 16:o + 20, :128], stg[o + 16:o + 20, 128:]], axis=0)
             put(S.at[1 - c, batch, :, j], R.at[batch, :, j], csem.at[batch], partner)
-            put(SZ.at[1 - c, 2 * j + batch], RZ.at[2 * j + batch], csem.at[2], partner)
+            put(SZ.at[1 - c, 4 * batch + j], RZ.at[4 * batch + j], csem.at[2], partner)
 
     sums(0, 0, 4)
     sums(1, 0, 2)
@@ -355,7 +360,7 @@
         third[batch].finish()
         fourth[batch].finish()
         for j in range(NZ // 2):
-            k = 2 * j + batch
+            k = 4 * batch + j
             for t in range(4):
                 zs[k, t] = Q[batch, t, j]
             d = lax.rem(k - z + NZ, NZ)
@@ -402,6 +407,7 @@
     alone(lambda: stage_one(1))
 
     alone(lambda: stage_one_middle(0))
+    alone(lambda: over.step(1))
 
     by_core(lambda b: _wait(zr.at[0:7 * (b + 1)], gsem.at[1, 1]))
     gz[...] = gp[...] + jnp.sum(zr[...].reshape(NZ - 1, 2, 8, 128), axis=0)
@@ -416,10 +422,9 @@
 
     by_core(spread)
 
-    alone(lambda: over.step(1))
     alone(lambda: stage_one_middle(1))
+    alone(lambda: over.step(2))
     alone(lambda: stage_two(0))
-    alone(lambda: over.step(2))
 
     def hand_over(b):
         n = b + 1
@@ -430,13 +435,13 @@
     by_core(lambda b: _wait(gr.at[0:16 * (2 - b)], gsem.at[3, 1]))
 
     events = {
-        (0, 2): lambda: stage_two(1),
-        (0, 5): lambda: stage_two_middle(0),
-        (0, 8): lambda: over.step(3),
-        (0, 11): lambda: stage_two_middle(1),
-        (0, 14): lambda: stage_three(0),
-        (1, 2): z_finish,
-        (1, 5): lambda: stage_three(1),
+        (0, 4): lambda: stage_two(1),
+        (0, 6): lambda: stage_two_middle(0),
+        (0, 7): lambda: over.step(3),
+        (0, 14): lambda: stage_two_middle(1),
+        (1, 1): lambda: stage_three(0),
+        (1, 3): z_finish,
+        (1, 6): lambda: stage_three(1),
     }
 
     def hook(half, k):

time: 46.6 us -> 45.8 us (0.983)
  Pallas kernels: 45.8 us -> 45 us
    pallas_call x1, Pallas kernels: 44.1 us -> 43.3 us  [local(): pl.pallas_call(functools.partial(kernel, rows * device_count), out_shape=...]
where the time goes in v5:
time: 45.8 us; the launch traced here: 45.6 us
  Pallas kernels  45 us (98%)
  between operations  0.64 us (1%)
    pallas_call x1, Pallas kernels, local(): pl.pallas_call(functools.partial(kernel, rows * device_count), out_shape=...  43.3 us
    pallas_call x1, Pallas kernels, local(): return pl.pallas_call(hand_on, out_shape=shapes)(*result)  1.68 us

profile of v5, /device:TPU:1, one launch (start us, length us, event | category | flops | bytes accessed | tf_op | source)
XLA Modules:
  0.0 45.6 jit_solution(12781232759169484542)
XLA Ops:
  0.6 43.3 %shard_map.59 = (bf16[512,256]{1,0:T(8,128)(2,1)}, f32[20,256]{1,0:T(8,128)}) custom-call(bf16[512,5120]{1,0:T(8,128)(2,1)} %counts.1, bf16[5120,256]{1,0:T(8,128)(2,1)} %basis.1, f32[40,128]{1,0:T(8,128)} %bitcast.2, f32[4,128]{1,0:T(4,128)} %bitcast.3), custom_call_target="tpu_custom_call" | custom-call | tf_op jit(solution)/shard_map/pallas_call | solution.py:495
  43.9 1.7 %shard_map.60 = (bf16[512,256]{1,0:T(8,128)(2,1)}, f32[20,256]{1,0:T(8,128)}) custom-call(bf16[512,256]{1,0:T(8,128)(2,1)} %get-tuple-element.4.a, f32[20,256]{1,0:T(8,128)} %get-tuple-element.5.b), custom_call_target="tpu_custom_call" | custom-call | tf_op jit(solution)/shard_map/pallas_call | solution.py:516

commit v6 on v5

--- a/solution.py
+++ b/solution.py
@@ -195,7 +195,7 @@
 def kernel(cells_all, counts, basis, scale, cells, cell_basis, gene_side,
            cbuf, bbuf, sbc, sk, wt, gl, gr, gp, zr, gz, gfull, w, tmp, stg, S, R, SZ, RZ, ZP, ZM, zt, zq,
            XP, XM, YP, YM, PX, PY, X2P, X2M, Y2P, Y2M, Q, zs, z3,
-           load_sem, gsem, csem, rsem, zsem, qsem):
+           high, low_part, load_sem, gsem, csem, rsem, zsem, qsem):
     sec = lax.axis_index("section")
     y = lax.axis_index("atlas")
     c = lax.rem(sec, 2)
@@ -422,6 +422,12 @@
 
     by_core(spread)
 
+    def split(value, at):
+        top_part = value.astype(jnp.bfloat16)
+        high[at, :] = top_part
+        low_part[at, :] = (value - top_part.astype(F32)).astype(jnp.bfloat16)
+
+    split(sk[...], slice(0, sk.shape[0]))
     alone(lambda: stage_one_middle(1))
     alone(lambda: over.step(2))
     alone(lambda: stage_two(0))
@@ -451,8 +457,6 @@
 
     inverse_factor(gfull, w, tmp, hook)
 
-    cell_basis[...] = dot(sk[...], w[...], ((1,), (1,))).astype(jnp.bfloat16)
-
     _wait(z3, zsem.at[1])
     _wait(zq.at[1:16], qsem.at[11])
     own = zs[z] + jnp.sum(z3[...], axis=0)
@@ -460,8 +464,18 @@
     mid = jnp.concatenate([own[2], own[3]], axis=1)
     rest = jnp.sum(zq[...], axis=0)
     low = jnp.concatenate([rest, pltpu.roll(rest, 4, 0)], axis=1)
-    side = dot(jnp.concatenate([top, mid, low], axis=0), w[...], ((1,), (1,)))
-    gene_side[...] = side[:20]
+    rows = sk.shape[0]
+    split(jnp.concatenate([top, mid, low, jnp.zeros_like(low)], axis=0), slice(rows, rows + 32))
+    factor = w[...]
+    factor_high = factor.astype(jnp.bfloat16)
+    factor_low = (factor - factor_high.astype(F32)).astype(jnp.bfloat16)
+
+    def times(a, b):
+        return lax.dot_general(a, b, (((1,), (1,)), ((), ())), preferred_element_type=F32)
+
+    both = times(high[...], factor_high) + (times(high[...], factor_low) + times(low_part[...], factor_high))
+    cell_basis[...] = both[:rows].astype(jnp.bfloat16)
+    gene_side[...] = both[rows:rows + 20]
 
     def drain(b):
         _wait(gr.at[0:47 - b], gsem.at[0, 0])
@@ -509,6 +523,7 @@
             vm(2, 2, 4, 4, 8, 128), vm(2, 2, 4, 4, 8, 128),
             vm(2, 3, 4, 8, 128), vm(2, 3, 4, 8, 128), vm(2, 3, 4, 8, 128), vm(2, 3, 4, 8, 128),
             vm(2, 4, 4, 8, 128), vm(NZ, 4, 8, 128), vm(NZ - 1, 4, 8, 128),
+            pltpu.VMEM((rows + 32, 256), jnp.bfloat16), pltpu.VMEM((rows + 32, 256), jnp.bfloat16),
             dma((2, CHUNKS)), dma((4, 2)), dma((3, 2)), dma((2, 4, 8)), dma((2,)), dma((12,)),
         ],
         compiler_params=pltpu.CompilerParams(collective_id=0, has_side_effects=True, vmem_limit_bytes=60 << 20),

time: 45.8 us -> 45.3 us (0.989)
  Pallas kernels: 45 us -> 44.5 us
    pallas_call x1, Pallas kernels: 43.3 us -> 42.8 us  [local(): pl.pallas_call(functools.partial(kernel, rows * device_count), out_shape=...]
where the time goes in v6:
time: 45.3 us; the launch traced here: 45.1 us
  Pallas kernels  44.5 us (98%)
  between operations  0.64 us (1%)
    pallas_call x1, Pallas kernels, local(): pl.pallas_call(functools.partial(kernel, rows * device_count), out_shape=...  42.8 us
    pallas_call x1, Pallas kernels, local(): return pl.pallas_call(hand_on, out_shape=shapes)(*result)  1.68 us

profile of v6, /device:TPU:1, one launch (start us, length us, event | category | flops | bytes accessed | tf_op | source)
XLA Modules:
  0.0 45.1 jit_solution(16715990736947550449)
XLA Ops:
  0.6 42.8 %shard_map.59 = (bf16[512,256]{1,0:T(8,128)(2,1)}, f32[20,256]{1,0:T(8,128)}) custom-call(bf16[512,5120]{1,0:T(8,128)(2,1)} %counts.1, bf16[5120,256]{1,0:T(8,128)(2,1)} %basis.1, f32[40,128]{1,0:T(8,128)} %bitcast.2, f32[4,128]{1,0:T(4,128)} %bitcast.3), custom_call_target="tpu_custom_call" | custom-call | tf_op jit(solution)/shard_map/pallas_call | solution.py:509
  43.4 1.7 %shard_map.60 = (bf16[512,256]{1,0:T(8,128)(2,1)}, f32[20,256]{1,0:T(8,128)}) custom-call(bf16[512,256]{1,0:T(8,128)(2,1)} %get-tuple-element.4.a, f32[20,256]{1,0:T(8,128)} %get-tuple-element.5.b), custom_call_target="tpu_custom_call" | custom-call | tf_op jit(solution)/shard_map/pallas_call | solution.py:531

commit v7 on v6

--- a/solution.py
+++ b/solution.py
@@ -275,10 +275,9 @@
         wt[rows, :] = (value * factor).astype(jnp.bfloat16)
 
     gram = dot(sk[...], sk[...], ((0,), (0,))) * (1.0 / cells_all)
-    for i in range(16):
-        gl[i, 0] = gram[8 * i:8 * i + 8, :128]
-        gl[i, 1] = gram[128 + 8 * i:136 + 8 * i, :128]
-        gl[i, 2] = gram[128 + 8 * i:136 + 8 * i, 128:]
+    gl[:, 0] = gram[:128, :128].reshape(16, 8, 128)
+    gl[:, 1] = gram[128:, :128].reshape(16, 8, 128)
+    gl[:, 2] = gram[128:, 128:].reshape(16, 8, 128)
 
     pl.semaphore_wait(barrier, PLANE - 1 + NZ - 1)
 
@@ -442,8 +441,8 @@
 
     events = {
         (0, 4): lambda: stage_two(1),
-        (0, 6): lambda: stage_two_middle(0),
-        (0, 7): lambda: over.step(3),
+        (0, 5): lambda: over.step(3),
+        (0, 7): lambda: stage_two_middle(0),
         (0, 14): lambda: stage_two_middle(1),
         (1, 1): lambda: stage_three(0),
         (1, 3): z_finish,

time: 45.3 us -> 45.5 us (level)
  no operation moved by 1% of the time
where the time goes in v7:
time: 45.5 us; the launch traced here: 45.3 us
  Pallas kernels  44.7 us (98%)
  between operations  0.64 us (1%)
    pallas_call x1, Pallas kernels, local(): pl.pallas_call(functools.partial(kernel, rows * device_count), out_shape=...  43 us
    pallas_call x1, Pallas kernels, local(): return pl.pallas_call(hand_on, out_shape=shapes)(*result)  1.68 us

profile of v7, /device:TPU:1, one launch (start us, length us, event | category | flops | bytes accessed | tf_op | source)
XLA Modules:
  0.0 45.3 jit_solution(15744945892197433411)
XLA Ops:
  0.6 43.0 %shard_map.59 = (bf16[512,256]{1,0:T(8,128)(2,1)}, f32[20,256]{1,0:T(8,128)}) custom-call(bf16[512,5120]{1,0:T(8,128)(2,1)} %counts.1, bf16[5120,256]{1,0:T(8,128)(2,1)} %basis.1, f32[40,128]{1,0:T(8,128)} %bitcast.2, f32[4,128]{1,0:T(4,128)} %bitcast.3), custom_call_target="tpu_custom_call" | custom-call | tf_op jit(solution)/shard_map/pallas_call | solution.py:508
  43.6 1.7 %shard_map.60 = (bf16[512,256]{1,0:T(8,128)(2,1)}, f32[20,256]{1,0:T(8,128)}) custom-call(bf16[512,256]{1,0:T(8,128)(2,1)} %get-tuple-element.4.a, f32[20,256]{1,0:T(8,128)} %get-tuple-element.5.b), custom_call_target="tpu_custom_call" | custom-call | tf_op jit(solution)/shard_map/pallas_call | solution.py:530
